TPU v7x, 256 devices: a whole 4x4x8 slice. The times are simulated.
256 devices in a mesh: dp: 32 (over z, x), proto: 8 (over y, core).
Axes of the slice: x: 4, y: 4, z: 8, core: 2. Of those that a mesh axis runs over, the one named last changes fastest.
Arguments:
- centroids: bfloat16 [131072, 768], P(('dp', 'proto')), may hold values from -1 to 1
- queries: bfloat16 [4096, 768], P('dp'), may hold values from -40 to 40
- positive: int32 [4096], P('dp'), may hold values from 0 to 131071
- members: bfloat16 [32, 32, 8, 16, 768], P('dp'), may hold values from -0.29882812 to 0.29882812
- member_slot: int32 [32, 32, 8, 16], P('dp'), may hold values from 0 to 511
- block_count: int32 [32, 32, 8], P('dp'), may hold values from 0 to 16, as said below
Outputs:
- concentration: float32 [131072], P(('dp', 'proto'))
- loss: float32 [4096], P('dp')
- query_grad: bfloat16 [4096, 768], P('dp')
Inputs may be any that keep to these rules, and one draw needn't show every extreme that they name: `block_count`: some block is full from every source group; the used slots come first in each block.
All inputs are finite; a program needn't handle non-finite values.
Results may differ from a plain program's by a relative error of at most 0.0056.
Values may be sent and summed in bfloat16 or wider, within the bound.
A program may use at most 128 MiB of HBM per device.

v0:
```python
import jax
import jax.numpy as jnp
from jax import lax
from jax.sharding import PartitionSpec as P


def on_device(centroids, queries, positive, members, member_slot, block_count):
    width = centroids.shape[1]
    cent_local = centroids.shape[0]
    q_local = queries.shape[0]
    column = lax.axis_index("proto")
    flat_index = lax.axis_index("dp") * lax.axis_size("proto") + column
    member_mine = lax.dynamic_index_in_dim(members, column, 2, keepdims=False)
    slot_mine = lax.dynamic_index_in_dim(member_slot, column, 2, keepdims=False)
    count_mine = lax.dynamic_index_in_dim(block_count, column, 2, keepdims=False)
    arrived, arrived_slot, arrived_count = (
        lax.all_to_all(member_mine, "dp", split_axis=1, concat_axis=0, tiled=True),
        lax.all_to_all(slot_mine, "dp", split_axis=1, concat_axis=0, tiled=True),
        lax.all_to_all(count_mine, "dp", split_axis=1, concat_axis=0, tiled=True),
    )
    slots_per = arrived.shape[2]
    member_rows = arrived.reshape(-1, width)
    slot_flat = arrived_slot.reshape(-1)
    valid = (
        (jnp.arange(slots_per, dtype=jnp.int32)[None, None, :] < arrived_count[:, :, None])
        .astype(jnp.float32)
        .reshape(-1)
    )
    picked = jnp.take(centroids, slot_flat, axis=0).astype(jnp.float32)
    distance = jnp.sqrt(jnp.sum((member_rows.astype(jnp.float32) - picked) ** 2, axis=1) + 1e-06)
    onehot = (jnp.arange(cent_local, dtype=jnp.int32)[:, None] == slot_flat[None, :]).astype(
        jnp.float32
    )
    total = jnp.dot(onehot, distance * valid, precision=lax.Precision.HIGHEST)
    counted = jnp.dot(onehot, valid, precision=lax.Precision.HIGHEST)
    concentration = (total + 1.0) / ((counted + 1.0) * jnp.log(counted + 10.0))
    inverse = 1.0 / concentration
    all_queries, all_positive = (
        lax.all_gather(queries, "dp", axis=0, tiled=True),
        lax.all_gather(positive, "dp", axis=0, tiled=True),
    )
    scores = (
        lax.dot_general(
            all_queries, centroids, (((1,), (1,)), ((), ())), preferred_element_type=jnp.float32
        )
        * inverse[None, :]
    )
    local_positive = all_positive - flat_index * cent_local
    positive_hit = (
        jnp.arange(cent_local, dtype=jnp.int32)[None, :] == local_positive[:, None]
    ).astype(jnp.float32)
    target_part = jnp.sum(scores * positive_hit, axis=1)
    local_max = jnp.max(scores, axis=1)
    row_max = lax.pmax(local_max, ("dp", "proto"))
    local_sum = jnp.sum(jnp.exp(scores - row_max[:, None]), axis=1)
    row_sum, target = lax.psum((local_sum, target_part), ("dp", "proto"))
    loss_all = row_max + jnp.log(row_sum) - target
    loss_mine = lax.dynamic_slice_in_dim(loss_all, lax.axis_index("dp") * q_local, q_local)
    probs = jnp.exp(scores - row_max[:, None]) / row_sum[:, None]
    weight = ((probs - positive_hit) * inverse[None, :]).astype(jnp.bfloat16)
    partial_rows = lax.psum_scatter(
        jnp.dot(weight, centroids, preferred_element_type=jnp.float32),
        "dp",
        scatter_dimension=0,
        tiled=True,
    )
    summed = lax.psum(partial_rows, "proto")
    return (concentration, loss_mine, summed.astype(jnp.bfloat16))


def solution(mesh):
    placed = (
        P(("dp", "proto"), None),
        P("dp", None),
        P("dp"),
        P("dp", None, None, None, None),
        P("dp", None, None, None),
        P("dp", None, None),
    )
    return jax.shard_map(
        on_device,
        mesh=mesh,
        in_specs=placed,
        out_specs=(P(("dp", "proto")), P("dp"), P("dp", None)),
        check_vma=False,
    )
```

profile of v0, /device:TPU:2, one launch (start us, length us, event | category | flops | bytes accessed | tf_op | source)
XLA Modules:
  0.0 548.8 jit_solution(13499479848178516080)
XLA Ops:
  7.2 0.7 all-gather.3.cloned.1.call-update
  7.9 0.7 constant_dynamic-slice_fusion
  8.6 0.7 copy.28
  9.3 11.6 %all-to-all-start.1 = ((s32[1,32,1]{2,0,1:T(1,128)}), s32[1,32,1]{2,0,1:T(1,128)S(1)}, u32[]{:S(2)}, u32[]{:S(2)}) async-start(s32[1,32,1]{2,0,1:T(1,128)} %copy.28), calls=%async_computation.1 | async-start | bytes 32768 | tf_op jit(solution)/shard_map/all_to_all | solution.py:19
  20.9 0.7 constant_dynamic-slice_fusion.1
  21.6 0.7 copy.23
  22.3 7.1 %all-to-all-done.1 = s32[1,32,1]{2,0,1:T(1,128)S(1)} async-done(((s32[1,32,1]{2,0,1:T(1,128)}), s32[1,32,1]{2,0,1:T(1,128)S(1)}, u32[]{:S(2)}, u32[]{:S(2)}) %all-to-all-start.1) | async-done | bytes 160 | tf_op jit(solution)/shard_map/all_to_all | solution.py:19
  29.4 4.9 all-to-all-start
  34.3 2.1 dynamic-slice_bitcast_fusion
  36.4 6.6 %all-to-all-done = s32[1,32,16]{2,0,1:T(1,128)S(1)} async-done(((s32[1,32,16]{2,0,1:T(1,128)}), s32[1,32,16]{2,0,1:T(1,128)S(1)}, u32[]{:S(2)}, u32[]{:S(2)}) %all-to-all-start) | async-done | bytes 2080 | tf_op jit(solution)/shard_map/all_to_all | solution.py:18
  43.0 4.9 all-to-all-start.2
  48.0 49.9 %all-gather = s32[32,1,128]{2,1,0:T(1,128)S(1)} all-gather(s32[1,1,128]{2,1,0:T(1,128)} %bitcast.42), channel_id=1, replica_groups=mesh['dp'=32,'proto'=8] {'dp'}, dimensions={0}, use_global_device_ids=true | all-gather | bytes 16896 | tf_op jit(solution)/shard_map/all_gather | solution.py:40
  97.9 0.7 reduce.4
  98.6 0.1 lt.61
  98.7 0.1 reshape.139
  98.8 0.1 reshape.124
  98.9 0.5 broadcast.91
  99.4 0.7 reduce.9
  100.3 0.1 copy.26
  100.4 2.0 gather_fusion
  102.4 0.3 fusion.2
  102.7 0.5 multiply_reduce_fusion.1
  103.4 0.6 fusion.3
  103.9 0.6 add_divide_fusion
  104.5 8.4 %multiply_reduce_fusion = (f32[4096]{0:T(1024)S(1)}, f32[4096,512]{0,1:T(8,128)}) fusion(f32[512]{0:T(512)S(1)} %get-tuple-element.7, bf16[4096,768]{1,0:T(8,128)(2,1)} %all-gather.3.cloned.1.call-done, bf16[512,768]{1,0:T(8,128)(2,1)S(1)} %copy-done), kind=kOutput, calls=%fused_computation.6 | convolution fusion | flops 3225415680 | bytes 15484928 | tf_op jit(solution)/shard_map/dot_general | solution.py:43
  112.9 73.2 %pmax.7 = f32[4096]{0:T(1024)S(1)} all-reduce(f32[4096]{0:T(1024)S(1)} %get-tuple-element.9), channel_id=1, replica_groups=mesh['dp'=32,'proto'=8] {'dp','proto'}, use_global_device_ids=true, to_apply=%region_2.3 | all-reduce | flops 4096 | bytes 32768 | tf_op jit(solution)/shard_map/pmax | solution.py:54
  186.1 5.0 fusion
  191.1 74.7 %all-reduce = (f32[4096]{0:T(1024)S(1)}, f32[4096]{0:T(1024)S(1)}) all-reduce(f32[4096]{0:T(1024)S(1)} %get-tuple-element.4, f32[4096]{0:T(1024)S(1)} %get-tuple-element.3), channel_id=1, replica_groups=mesh['dp'=32,'proto'=8] {'dp','proto'}, use_global_device_ids=true, to_apply=%region_6.7 | all-reduce | flops 8192 | bytes 65536 | tf_op jit(solution)/shard_map/psum | solution.py:56
  265.8 13.1 %fusion.1 = f32[4096,768]{1,0:T(8,128)} fusion(bf16[512,768]{1,0:T(8,128)(2,1)S(1)} %copy-done, f32[4096,512]{0,1:T(8,128)} %get-tuple-element.10, f32[4096]{0:T(1024)S(1)} %get-tuple-element.6, s32[4096]{0:T(1024)S(1)} %bitcast.36, f32[4096]{0:T(1024)S(1)} %pmax.7, f32[512]{0:T(512)S(1)} %get-tuple-element.7), kind=kOutput, calls=%fused_computation.7 | convolution fusion | flops 3238002688 | bytes 21809152 | tf_op jit(solution)/shard_map/dot_general | solution.py:62
  278.9 0.6 dynamic-slice_subtract_fusion
  279.5 233.8 %reduce-scatter.2.cloned.1.call-done = f32[128,768]{1,0:T(8,128)} async-done(((f32[4096,768]{1,0:T(8,128)}), f32[128,768]{1,0:T(8,128)}) %reduce-scatter.2.cloned.1.call-update) | async-done | bytes 393232 | tf_op jit(solution)/shard_map/reduce_scatter | solution.py:61
  513.2 28.7 %all-reduce.2 = bf16[128,768]{1,0:T(8,128)(2,1)} all-reduce(f32[128,768]{1,0:T(8,128)} %reduce-scatter.2.cloned.1.call-done), channel_id=1, replica_groups=mesh['dp'=32,'proto'=8] {'proto'}, use_global_device_ids=true, to_apply=%region_8.9 | all-reduce | flops 98304 | bytes 589824 | tf_op jit(solution)/shard_map/psum | solution.py:67
  (17 shorter events, 0.5 us)
Async XLA Ops:
  7.2 93.2 %copy-start = (bf16[512,768]{1,0:T(8,128)(2,1)S(1)}, bf16[512,768]{1,0:T(8,128)(2,1)}, u32[]{:S(2)}) copy-start(bf16[512,768]{1,0:T(8,128)(2,1)} %param.6) | copy-start | bytes 2359300
  7.2 97.3 %all-gather.3.cloned.1.call-start = ((), (), s32[]{:S(2)}) async-start(), calls=%async_computation.4 | async-start | bytes 6488064 | tf_op jit(solution)/shard_map/all_gather | solution.py:39
  9.3 20.1 %all-to-all-start.1 = ((s32[1,32,1]{2,0,1:T(1,128)}), s32[1,32,1]{2,0,1:T(1,128)S(1)}, u32[]{:S(2)}, u32[]{:S(2)}) async-start(s32[1,32,1]{2,0,1:T(1,128)} %copy.28), calls=%async_computation.1 | async-start | bytes 32768 | tf_op jit(solution)/shard_map/all_to_all | solution.py:19
  29.4 13.6 %all-to-all-start = ((s32[1,32,16]{2,0,1:T(1,128)}), s32[1,32,16]{2,0,1:T(1,128)S(1)}, u32[]{:S(2)}, u32[]{:S(2)}) async-start(s32[1,32,16]{2,0,1:T(1,128)} %bitcast), calls=%async_computation | async-start | bytes 32768 | tf_op jit(solution)/shard_map/all_to_all | solution.py:18
  43.0 59.7 %all-to-all-start.2 = ((bf16[1,32,16,768]{3,2,0,1:T(8,128)(2,1)}), bf16[1,32,16,768]{3,2,0,1:T(8,128)(2,1)S(1)}, u32[]{:S(2)}, u32[]{:S(2)}) async-start(bf16[1,32,16,768]{3,2,0,1:T(8,128)(2,1)} %dynamic-slice_bitcast_fusion), calls=%async_computation.2 | async-start | bytes 1572864 | tf_op jit(solution)/shard_map/all_to_all | solution.py:17
  48.0 465.3 %reduce-scatter.2.cloned.1.call-start = ((), (), s32[]{:S(2)}) async-start(), calls=%async_computation.5 | async-start | bytes 12976128 | tf_op jit(solution)/shard_map/reduce_scatter | solution.py:61
Sparse Core Ops, SparseCore 0:
  10.6 91.8 all-gather.2
  279.0 234.1 reduce-scatter.1
where the time goes:
time: 550 us; the launch traced here: 549 us
  waiting for transfers between devices  248 us (45%)
  blocking collectives  226 us (41%)
  matrix products  22.3 us (4%)
  starting transfers between devices  21.5 us (4%)
  between operations  14.2 us (3%)
  other arithmetic  8.13 us (1%)
  local copies, waits for them, and re-layouts  7.99 us (1%)
    reduce_scatter x1, waiting for transfers between devices, on_device(): lax.psum_scatter(jnp.dot(weight, centroids, preferred_element_type=jnp.fl...  234 us
    psum x1, blocking collectives, on_device(): row_sum, target = lax.psum((local_sum, target_part), ('dp', 'proto'))  74.7 us
    pmax x1, blocking collectives, on_device(): row_max = lax.pmax(local_max, ('dp', 'proto'))  73.2 us
    all_gather x1, blocking collectives, on_device(): lax.all_gather(positive, 'dp', axis=0, tiled=True)  49.9 us
    psum x1, blocking collectives, on_device(): summed = lax.psum(partial_rows, 'proto')  28.7 us
    dot_general x1, matrix products, on_device(): jnp.dot(weight, centroids, preferred_element_type=jnp.float32)  13.1 us
    all_to_all x1, starting transfers between devices, on_device(): lax.all_to_all(count_mine, 'dp', split_axis=1, concat_axis=0, tiled=True)  11.6 us
  transfers between devices with their start and end apart: 5, of which 3 were waited for; matrix products, arithmetic and copies ran while one was open for 2% of the time, Pallas kernels for 0%

commit v1 on v0

--- a/solution.py
+++ b/solution.py
@@ -53,7 +53,7 @@
     local_max = jnp.max(scores, axis=1)
     row_max = lax.pmax(local_max, ("dp", "proto"))
     local_sum = jnp.sum(jnp.exp(scores - row_max[:, None]), axis=1)
-    row_sum, target = lax.psum((local_sum, target_part), ("dp", "proto"))
+    row_sum, target = lax.psum(lax.psum((local_sum, target_part), "proto"), "dp")
     loss_all = row_max + jnp.log(row_sum) - target
     loss_mine = lax.dynamic_slice_in_dim(loss_all, lax.axis_index("dp") * q_local, q_local)
     probs = jnp.exp(scores - row_max[:, None]) / row_sum[:, None]

time: 550 us -> 638 us (1.16)
  blocking collectives: 226 us -> 312 us
    psum x1 -> x2, blocking collectives: 74.7 us -> 161 us  [the longest x1 136 us: on_device(): lax.psum(lax.psum((local_sum, target_part), 'proto'), 'dp')]
where the time goes in v1:
time: 638 us; the launch traced here: 637 us
  blocking collectives  312 us (49%)
  waiting for transfers between devices  251 us (39%)
  matrix products  22.3 us (3%)
  starting transfers between devices  21.5 us (3%)
  between operations  14.2 us (2%)
  other arithmetic  8.13 us (1%)
  local copies, waits for them, and re-layouts  7.99 us (1%)
    reduce_scatter x1, waiting for transfers between devices, on_device(): lax.psum_scatter(jnp.dot(weight, centroids, preferred_element_type=jnp.fl...  236 us
    psum x1, blocking collectives, on_device(): lax.psum(lax.psum((local_sum, target_part), 'proto'), 'dp')  136 us
    pmax x1, blocking collectives, on_device(): row_max = lax.pmax(local_max, ('dp', 'proto'))  73.2 us
    all_gather x1, blocking collectives, on_device(): lax.all_gather(positive, 'dp', axis=0, tiled=True)  49.9 us
    psum x1, blocking collectives, on_device(): summed = lax.psum(partial_rows, 'proto')  28.7 us
    psum x1, blocking collectives, on_device(): lax.psum((local_sum, target_part), 'proto')  24.8 us
    dot_general x1, matrix products, on_device(): jnp.dot(weight, centroids, preferred_element_type=jnp.float32)  13.1 us
  transfers between devices with their start and end apart: 5, of which 3 were waited for; matrix products, arithmetic and copies ran while one was open for 2% of the time, Pallas kernels for 0%

profile of v1, /device:TPU:2, one launch (start us, length us, event | category | flops | bytes accessed | tf_op | source)
XLA Modules:
  0.0 637.2 jit_solution(352925320475696971)
XLA Ops:
  7.2 0.7 all-gather.3.cloned.1.call-update
  7.9 0.7 constant_dynamic-slice_fusion
  8.6 0.7 copy.28
  9.3 11.6 %all-to-all-start.1 = ((s32[1,32,1]{2,0,1:T(1,128)}), s32[1,32,1]{2,0,1:T(1,128)S(1)}, u32[]{:S(2)}, u32[]{:S(2)}) async-start(s32[1,32,1]{2,0,1:T(1,128)} %copy.28), calls=%async_computation.1 | async-start | bytes 32768 | tf_op jit(solution)/shard_map/all_to_all | solution.py:19
  20.9 0.7 constant_dynamic-slice_fusion.1
  21.6 0.7 copy.23
  22.3 7.1 %all-to-all-done.1 = s32[1,32,1]{2,0,1:T(1,128)S(1)} async-done(((s32[1,32,1]{2,0,1:T(1,128)}), s32[1,32,1]{2,0,1:T(1,128)S(1)}, u32[]{:S(2)}, u32[]{:S(2)}) %all-to-all-start.1) | async-done | bytes 160 | tf_op jit(solution)/shard_map/all_to_all | solution.py:19
  29.4 4.9 all-to-all-start
  34.3 2.1 dynamic-slice_bitcast_fusion
  36.4 6.6 %all-to-all-done = s32[1,32,16]{2,0,1:T(1,128)S(1)} async-done(((s32[1,32,16]{2,0,1:T(1,128)}), s32[1,32,16]{2,0,1:T(1,128)S(1)}, u32[]{:S(2)}, u32[]{:S(2)}) %all-to-all-start) | async-done | bytes 2080 | tf_op jit(solution)/shard_map/all_to_all | solution.py:18
  43.0 4.9 all-to-all-start.2
  48.0 49.9 %all-gather = s32[32,1,128]{2,1,0:T(1,128)S(1)} all-gather(s32[1,1,128]{2,1,0:T(1,128)} %bitcast.42), channel_id=1, replica_groups=mesh['dp'=32,'proto'=8] {'dp'}, dimensions={0}, use_global_device_ids=true | all-gather | bytes 16896 | tf_op jit(solution)/shard_map/all_gather | solution.py:40
  97.9 0.7 reduce.4
  98.6 0.1 lt.61
  98.7 0.1 reshape.139
  98.9 0.5 broadcast.91
  99.4 0.7 reduce.9
  100.3 0.1 copy.26
  100.4 2.0 gather_fusion
  102.4 0.3 fusion.2
  102.7 0.5 multiply_reduce_fusion.1
  103.4 0.6 fusion.3
  103.9 0.6 add_divide_fusion
  104.5 8.4 %multiply_reduce_fusion = (f32[4096]{0:T(1024)S(1)}, f32[4096,512]{0,1:T(8,128)}) fusion(f32[512]{0:T(512)S(1)} %get-tuple-element.9, bf16[4096,768]{1,0:T(8,128)(2,1)} %all-gather.3.cloned.1.call-done, bf16[512,768]{1,0:T(8,128)(2,1)S(1)} %copy-done), kind=kOutput, calls=%fused_computation.6 | convolution fusion | flops 3225415680 | bytes 15484928 | tf_op jit(solution)/shard_map/dot_general | solution.py:43
  112.9 73.2 %pmax.7 = f32[4096]{0:T(1024)S(1)} all-reduce(f32[4096]{0:T(1024)S(1)} %get-tuple-element.11), channel_id=1, replica_groups=mesh['dp'=32,'proto'=8] {'dp','proto'}, use_global_device_ids=true, to_apply=%region_2.3 | all-reduce | flops 4096 | bytes 32768 | tf_op jit(solution)/shard_map/pmax | solution.py:54
  186.1 5.0 fusion
  191.1 24.8 %all-reduce.1 = (f32[4096]{0:T(1024)S(1)}, f32[4096]{0:T(1024)S(1)}) all-reduce(f32[4096]{0:T(1024)S(1)} %get-tuple-element.4, f32[4096]{0:T(1024)S(1)} %get-tuple-element.3), channel_id=1, replica_groups=mesh['dp'=32,'proto'=8] {'proto'}, use_global_device_ids=true, to_apply=%region_7.8 | all-reduce | flops 8192 | bytes 65536 | tf_op jit(solution)/shard_map/psum | solution.py:56
  215.9 135.8 %all-reduce = (f32[4096]{0:T(1024)S(1)}, f32[4096]{0:T(1024)S(1)}) all-reduce(f32[4096]{0:T(1024)S(1)} %get-tuple-element.7, f32[4096]{0:T(1024)S(1)} %get-tuple-element.8), channel_id=1, replica_groups=mesh['dp'=32,'proto'=8] {'dp'}, use_global_device_ids=true, to_apply=%region_8.9 | all-reduce | flops 8192 | bytes 65536 | tf_op jit(solution)/shard_map/psum | solution.py:56
  351.7 13.1 %fusion.1 = f32[4096,768]{1,0:T(8,128)} fusion(bf16[512,768]{1,0:T(8,128)(2,1)S(1)} %copy-done, f32[4096,512]{0,1:T(8,128)} %get-tuple-element.12, f32[4096]{0:T(1024)S(1)} %get-tuple-element.6, s32[4096]{0:T(1024)S(1)} %bitcast.36, f32[4096]{0:T(1024)S(1)} %pmax.7, f32[512]{0:T(512)S(1)} %get-tuple-element.9), kind=kOutput, calls=%fused_computation.7 | convolution fusion | flops 3238002688 | bytes 21809152 | tf_op jit(solution)/shard_map/dot_general | solution.py:62
  364.8 0.6 dynamic-slice_subtract_fusion
  365.4 236.2 %reduce-scatter.2.cloned.1.call-done = f32[128,768]{1,0:T(8,128)} async-done(((f32[4096,768]{1,0:T(8,128)}), f32[128,768]{1,0:T(8,128)}) %reduce-scatter.2.cloned.1.call-update) | async-done | bytes 393232 | tf_op jit(solution)/shard_map/reduce_scatter | solution.py:61
  601.6 28.7 %all-reduce.3 = bf16[128,768]{1,0:T(8,128)(2,1)} all-reduce(f32[128,768]{1,0:T(8,128)} %reduce-scatter.2.cloned.1.call-done), channel_id=1, replica_groups=mesh['dp'=32,'proto'=8] {'proto'}, use_global_device_ids=true, to_apply=%region_10.11 | all-reduce | flops 98304 | bytes 589824 | tf_op jit(solution)/shard_map/psum | solution.py:67
  (18 shorter events, 0.5 us)
Async XLA Ops:
  7.2 93.2 %copy-start = (bf16[512,768]{1,0:T(8,128)(2,1)S(1)}, bf16[512,768]{1,0:T(8,128)(2,1)}, u32[]{:S(2)}) copy-start(bf16[512,768]{1,0:T(8,128)(2,1)} %param.6) | copy-start | bytes 2359300
  7.2 97.3 %all-gather.3.cloned.1.call-start = ((), (), s32[]{:S(2)}) async-start(), calls=%async_computation.4 | async-start | bytes 6488064 | tf_op jit(solution)/shard_map/all_gather | solution.py:39
  9.3 20.1 %all-to-all-start.1 = ((s32[1,32,1]{2,0,1:T(1,128)}), s32[1,32,1]{2,0,1:T(1,128)S(1)}, u32[]{:S(2)}, u32[]{:S(2)}) async-start(s32[1,32,1]{2,0,1:T(1,128)} %copy.28), calls=%async_computation.1 | async-start | bytes 32768 | tf_op jit(solution)/shard_map/all_to_all | solution.py:19
  29.4 13.6 %all-to-all-start = ((s32[1,32,16]{2,0,1:T(1,128)}), s32[1,32,16]{2,0,1:T(1,128)S(1)}, u32[]{:S(2)}, u32[]{:S(2)}) async-start(s32[1,32,16]{2,0,1:T(1,128)} %bitcast), calls=%async_computation | async-start | bytes 32768 | tf_op jit(solution)/shard_map/all_to_all | solution.py:18
  43.0 59.7 %all-to-all-start.2 = ((bf16[1,32,16,768]{3,2,0,1:T(8,128)(2,1)}), bf16[1,32,16,768]{3,2,0,1:T(8,128)(2,1)S(1)}, u32[]{:S(2)}, u32[]{:S(2)}) async-start(bf16[1,32,16,768]{3,2,0,1:T(8,128)(2,1)} %dynamic-slice_bitcast_fusion), calls=%async_computation.2 | async-start | bytes 1572864 | tf_op jit(solution)/shard_map/all_to_all | solution.py:17
  48.0 553.7 %reduce-scatter.2.cloned.1.call-start = ((), (), s32[]{:S(2)}) async-start(), calls=%async_computation.5 | async-start | bytes 12976128 | tf_op jit(solution)/shard_map/reduce_scatter | solution.py:61
Sparse Core Ops, SparseCore 0:
  10.6 91.8 all-gather.2
  365.0 236.6 reduce-scatter.1
